TPU v7x, 32 devices: a whole 2x2x4 slice. The times are simulated.
32 devices in a mesh: req: 8 (over z, y), head: 4 (over x, core).
Axes of the slice: x: 2, y: 2, z: 4, core: 2. Of those that a mesh axis runs over, the one named last changes fastest.
Arguments:
- stream_in: bfloat16 [512, 2560], P('req'), may hold values from -6 to 6
- norm_gain: float32 [2560], replicated, may hold values from 0.25 to 1.75
- gate_weight: bfloat16 [2560, 5120], P(None, 'head'), may hold values from -0.125 to 0.125
- inner_weight: bfloat16 [2560, 5120], P(None, 'head'), may hold values from -0.125 to 0.125
- readwrite_weight: bfloat16 [2560, 256], replicated, may hold values from -0.125 to 0.125
- step_weight: bfloat16 [2560, 80], P(None, 'head'), may hold values from -0.125 to 0.125
- conv_inner: bfloat16 [4, 5120], P(None, 'head'), may hold values from -3 to 3
- conv_readwrite: bfloat16 [4, 256], replicated, may hold values from -3 to 3
- decay_log: float32 [80], P('head'), may hold values from 0 to 2.77
- step_bias: float32 [80], P('head'), may hold values from -4 to -1
- skip_gain: float32 [80], P('head'), may hold values from 0.5 to 1.5
- gate_gain: float32 [5120], P('head'), may hold values from 0.25 to 1.75
- out_weight: bfloat16 [5120, 2560], P('head'), may hold values from -0.078125 to 0.078125
- final_gain: float32 [2560], replicated, may hold values from 0.25 to 1.75
- embedding: bfloat16 [50304, 2560], P(('req', 'head')), may hold values from -0.375 to 0.375
- state_cache: bfloat16 [128, 80, 64, 128], P('req', 'head'), may hold values from -4 to 4
- window_inner: bfloat16 [128, 3, 5120], P('req', None, 'head'), may hold values from -6 to 6
- window_readwrite: bfloat16 [128, 3, 256], P('req'), may hold values from -6 to 6
- source_row: int32 [128], replicated, may hold values from 0 to 127, as said below
- lengths: int32 [128], P('req'), may hold values from 1 to 4, 320 in all
- draft_ids: int32 [512], replicated, may hold values from 0 to 50303
Outputs:
- state_after: bfloat16 [128, 80, 64, 128], P('req', 'head')
- tail_inner: bfloat16 [128, 3, 5120], P('req', None, 'head')
- tail_readwrite: bfloat16 [128, 3, 256], P('req')
- hidden_rms: float32 [512], P(('req', 'head'))
- top_logit: float32 [512], P(('req', 'head'))
- draft_logit: float32 [512], P(('req', 'head'))
Inputs may be any that keep to these rules, and one draw needn't show every extreme that they name: `source_row`: a permutation of the requests; of the 16 requests r * 16 to r * 16 + 15, exactly 2 have their stored row in each block of 16 rows. The first lengths[r] slots of request r are live.
All inputs are finite; a program needn't handle non-finite values. No bound on the sum of `lengths` on one device may be relied on, other than what follows from the above.
Results may differ from a plain program's by a relative error of at most 0.01.
Values may be sent and summed in bfloat16 or wider, within the bound.
No kernel may reach another device: no remote copies, remote signals or barrier semaphores. Data moves between devices by JAX's collectives and lax.ppermute only.
A program may use at most 320 MiB of HBM per device.

v0:
```python
import jax
import jax.numpy as jnp
from jax import lax
from jax.sharding import PartitionSpec as P

epsilon = 1e-05
lowest = -1e30


def rms_of(values):
    return jnp.sqrt(jnp.mean(values * values, axis=-1, keepdims=True) + epsilon)


def conv_silu(window, weight):
    taps = weight.shape[0]
    count = window.shape[1] - taps + 1
    total = jnp.zeros((window.shape[0], count, window.shape[2]), jnp.float32)
    for kernel_tap in range(taps):
        total = total + window[:, kernel_tap : kernel_tap + count].astype(jnp.float32) * weight[
            kernel_tap
        ].astype(jnp.float32)
    return jax.nn.silu(total).astype(jnp.bfloat16)


def last_rows(window, lengths, keep):
    places = jnp.arange(window.shape[1], dtype=jnp.int32)
    wide = window.astype(jnp.float32)
    picked = []
    for lag_index in range(keep):
        select = (places[None, :] == lengths[:, None] + lag_index).astype(jnp.float32)
        picked.append(jnp.sum(select[:, :, None] * wide, axis=1))
    return jnp.stack(picked, axis=1).astype(jnp.bfloat16)


def run_slots(state, inner, writes, reads, steps, decays, skip_gain):
    outputs = []
    for slot_index in range(inner.shape[1]):
        current = inner[:, slot_index].astype(jnp.float32)
        update = (steps[:, slot_index, :, None] * current)[..., None] * writes[
            :, slot_index, None, None, :
        ].astype(jnp.float32)
        state = decays[:, slot_index, :, None, None] * state + update
        value = jnp.einsum(
            "rhpn,rn->rhp",
            state,
            reads[:, slot_index].astype(jnp.float32),
            precision=lax.Precision.HIGHEST,
        )
        outputs.append(value + skip_gain[None, :, None] * current)
    return (state, jnp.stack(outputs, axis=1))


def on_device(
    stream_in,
    norm_gain,
    gate_weight,
    inner_weight,
    readwrite_weight,
    step_weight,
    conv_inner,
    conv_readwrite,
    decay_log,
    step_bias,
    skip_gain,
    gate_gain,
    out_weight,
    final_gain,
    embedding,
    state_cache,
    window_inner,
    window_readwrite,
    source_row,
    lengths,
    draft_ids,
):
    n_head = lax.axis_size("head")
    req_index = lax.axis_index("req")
    head_index = lax.axis_index("head")
    rows_dev = stream_in.shape[0]
    req_dev = lengths.shape[0]
    slots = rows_dev // req_dev
    all_req = source_row.shape[0]
    heads_dev = decay_log.shape[0]
    head_width = state_cache.shape[2]
    state_dim = state_cache.shape[3]
    inner_dev = inner_weight.shape[1]
    vocab_dev = embedding.shape[0]
    share = rows_dev // n_head
    first_req = req_index * req_dev
    takes_row = jnp.argsort(source_row)
    my_targets = lax.dynamic_slice_in_dim(takes_row, first_req, req_dev)
    send_order = jnp.argsort(my_targets)
    outgoing = (
        jnp.take(state_cache, send_order, axis=0),
        jnp.take(window_inner, send_order, axis=0),
        jnp.take(window_readwrite, send_order, axis=0),
    )
    arrived = (
        lax.all_to_all(outgoing[0], "req", split_axis=0, concat_axis=0, tiled=True),
        lax.all_to_all(outgoing[1], "req", split_axis=0, concat_axis=0, tiled=True),
        lax.all_to_all(outgoing[2], "req", split_axis=0, concat_axis=0, tiled=True),
    )
    my_sources = lax.dynamic_slice_in_dim(source_row, first_req, req_dev) // req_dev
    arrival_key = my_sources * all_req + first_req + jnp.arange(req_dev, dtype=jnp.int32)
    arrival_place = jnp.argsort(jnp.argsort(arrival_key))
    old_state = jnp.take(arrived[0], arrival_place, axis=0)
    old_inner = jnp.take(arrived[1], arrival_place, axis=0)
    old_readwrite = jnp.take(arrived[2], arrival_place, axis=0)
    stream = stream_in.astype(jnp.float32)
    normed = (stream / rms_of(stream) * norm_gain).astype(jnp.bfloat16)
    gate_val = jnp.dot(normed, gate_weight, preferred_element_type=jnp.float32).astype(jnp.bfloat16)
    inner_raw = jnp.dot(normed, inner_weight, preferred_element_type=jnp.float32).astype(
        jnp.bfloat16
    )
    readwrite_raw = jnp.dot(normed, readwrite_weight, preferred_element_type=jnp.float32).astype(
        jnp.bfloat16
    )
    step_raw = jnp.dot(normed, step_weight, preferred_element_type=jnp.float32).astype(jnp.bfloat16)
    full_inner = jnp.concatenate([old_inner, inner_raw.reshape(req_dev, slots, inner_dev)], axis=1)
    full_readwrite = jnp.concatenate(
        [old_readwrite, readwrite_raw.reshape(req_dev, slots, 2 * state_dim)], axis=1
    )
    inner_conv = conv_silu(full_inner, conv_inner)
    readwrite_conv = conv_silu(full_readwrite, conv_readwrite)
    taps = conv_inner.shape[0]
    tail_inner = last_rows(full_inner, lengths, taps - 1)
    tail_readwrite = last_rows(full_readwrite, lengths, taps - 1)
    live = (jnp.arange(slots, dtype=jnp.int32)[None, :] < lengths[:, None]).astype(jnp.float32)
    steps = (
        jax.nn.softplus(step_raw.astype(jnp.float32).reshape(req_dev, slots, heads_dev) + step_bias)
        * live[:, :, None]
    )
    decays = jnp.exp(-jnp.exp(decay_log) * steps)
    final_state, slot_out = run_slots(
        old_state.astype(jnp.float32),
        inner_conv.reshape(req_dev, slots, heads_dev, head_width),
        readwrite_conv[..., :state_dim],
        readwrite_conv[..., state_dim:],
        steps,
        decays,
        skip_gain,
    )
    state_after = final_state.astype(jnp.bfloat16)
    slot_values = slot_out.reshape(rows_dev, inner_dev)
    gated = slot_values * jax.nn.silu(gate_val.astype(jnp.float32))
    local_squares = jnp.sum(gated * gated, axis=1)
    total_squares = lax.psum(local_squares, "head")
    gated_normed = (
        gated / jnp.sqrt(total_squares[:, None] / (inner_dev * n_head) + epsilon) * gate_gain
    ).astype(jnp.bfloat16)
    live_tokens = live.reshape(rows_dev) > 0.5
    live_share = lax.dynamic_slice_in_dim(live_tokens, head_index * share, share)
    mixed = lax.psum(jnp.dot(gated_normed, out_weight, preferred_element_type=jnp.float32), "head")
    residual = stream + mixed
    scale = rms_of(residual)
    final_rows = (residual / scale * final_gain).astype(jnp.bfloat16)
    scale_share = lax.dynamic_slice_in_dim(scale[:, 0], head_index * share, share)
    hidden_rms = jnp.where(live_share, scale_share, 0.0)
    my_ids = lax.dynamic_slice_in_dim(draft_ids, req_index * rows_dev, rows_dev)
    start_rows = jnp.full((rows_dev,), lowest, jnp.float32)
    piece = lax.all_gather(embedding, "req", axis=0, tiled=True)
    logits = lax.dot_general(
        final_rows, piece, (((1,), (1,)), ((), ())), preferred_element_type=jnp.float32
    )
    spot = jnp.arange(piece.shape[0], dtype=jnp.int32)
    vocab_id = (spot // vocab_dev * n_head + head_index) * vocab_dev + spot % vocab_dev
    matched = jnp.where(my_ids[:, None] == vocab_id[None, :], logits, lowest)
    top_rows = jnp.maximum(start_rows, jnp.max(logits, axis=1))
    draft_rows = jnp.maximum(start_rows, jnp.max(matched, axis=1))
    top_rows, draft_rows = lax.pmax((top_rows, draft_rows), "head")
    top_share = lax.dynamic_slice_in_dim(top_rows, head_index * share, share)
    draft_share = lax.dynamic_slice_in_dim(draft_rows, head_index * share, share)
    top_logit = jnp.where(live_share, top_share, 0.0)
    draft_logit = jnp.where(live_share, draft_share, 0.0)
    return (state_after, tail_inner, tail_readwrite, hidden_rms, top_logit, draft_logit)


def solution(mesh):
    in_specs = (
        P("req", None),
        P(),
        P(None, "head"),
        P(None, "head"),
        P(),
        P(None, "head"),
        P(None, "head"),
        P(),
        P("head"),
        P("head"),
        P("head"),
        P("head"),
        P("head", None),
        P(),
        P(("req", "head"), None),
        P("req", "head", None, None),
        P("req", None, "head"),
        P("req", None, None),
        P(),
        P("req"),
        P(),
    )
    out_specs = (
        P("req", "head", None, None),
        P("req", None, "head"),
        P("req", None, None),
        P(("req", "head")),
        P(("req", "head")),
        P(("req", "head")),
    )
    return jax.shard_map(
        on_device, mesh=mesh, in_specs=in_specs, out_specs=out_specs, check_vma=False
    )
```

profile of v0, /device:TPU:0, one launch (start us, length us, event | category | flops | bytes accessed | tf_op | source)
XLA Modules:
  0.0 1580.2 jit_solution(14975383909090530984)
XLA Ops:
  8.0 3.3 sort.62
  11.3 0.1 dynamic_slice.21
  11.4 1.2 sort.63
  12.7 1.4 gather_fusion.4
  14.0 0.1 broadcast_select_fusion.5
  14.1 0.6 copy.59
  14.8 7.3 all-to-all-start.2
  22.0 1.8 gather_fusion.2
  23.9 0.1 broadcast_select_fusion.3
  23.9 0.7 copy.55
  24.7 6.1 gather_fusion
  30.8 6.0 all-to-all-start.1
  36.8 5.5 broadcast_select_fusion.1
  42.3 2.0 all-to-all-done.1
  44.3 4.6 all-to-all-start
  49.0 0.2 all-reduce.3.cloned.1.call-start
  49.2 0.2 fusion.19
  49.4 0.3 fusion.18
  49.7 0.1 copy.54
  49.8 0.4 convolution_convert_fusion.2
  50.2 4.2 convolution_convert_fusion.1
  54.5 0.1 iota_add_fusion
  54.5 1.2 sort.64
  55.8 1.2 sort.65
  57.1 0.1 convert_reduce_fusion.3
  57.2 0.1 broadcast_compare_fusion
  57.3 0.1 multiply_exponential_fusion
  57.4 0.6 gather_fusion.5
  58.0 0.1 broadcast_select_fusion.4
  58.2 0.7 gather_fusion.3
  58.9 0.1 broadcast_select_fusion.2
  59.1 0.2 multiply_convert_fusion.3
  59.3 0.3 reshape.339
  59.6 0.3 convert_multiply_fusion.11
  59.9 103.2 %all-to-all-done = bf16[16,20,64,128]{3,2,1,0:T(8,128)(2,1)} async-done(((bf16[16,20,64,128]{3,2,1,0:T(8,128)(2,1)}), bf16[16,20,64,128]{3,2,1,0:T(8,128)(2,1)}, u32[]{:S(2)}, u32[]{:S(2)}) %all-to-all-start) | async-done | bytes 5242912 | tf_op jit(solution)/shard_map/all_to_all | solution.py:99
  163.1 6.1 gather_fusion.1
  169.1 14.9 fusion
  184.0 17.5 %fusion.1 = f32[16,1,20,64]{3,1,2,0:T(1,128)S(1)} fusion(f32[16,128]{1,0:T(8,128)S(1)} %get-tuple-element.47, f32[16,20,64]{2,1,0:T(8,128)S(1)} %get-tuple-element.40, f32[16,128]{1,0:T(8,128)S(1)} %get-tuple-element.48, f32[16,20,64]{2,1,0:T(8,128)S(1)} %get-tuple-element.37, f32[16,20]{1,0:T(8,128)S(1)} %bitcast.138, f32[16,20]{1,0:T(8,128)S(1)} %bitcast.142, ...), kind=kOutput, calls=%fused_computation.11 | convolution fusion | flops 52428800 | bytes 5511696 | tf_op jit(solution)/shard_map/rhpn,rn->rhp/dot_general | solution.py:43
  201.5 20.6 %fusion.16 = f32[16,1,20,64]{3,1,2,0:T(1,128)S(1)} fusion(f32[16,128]{1,0:T(8,128)S(1)} %get-tuple-element.46, f32[16,20,64]{2,1,0:T(8,128)S(1)} %get-tuple-element.39, f32[16,128]{1,0:T(8,128)S(1)} %get-tuple-element.47, f32[16,20,64]{2,1,0:T(8,128)S(1)} %get-tuple-element.40, f32[16,128]{1,0:T(8,128)S(1)} %get-tuple-element.48, ...), kind=kOutput, calls=%fused_computation.28 | convolution fusion | flops 60293120 | bytes 5603088 | tf_op jit(solution)/shard_map/rhpn,rn->rhp/dot_general | solution.py:43
  222.1 23.6 %fusion.2 = f32[16,1,20,64]{3,1,2,0:T(1,128)S(1)} fusion(f32[16,128]{1,0:T(8,128)S(1)} %get-tuple-element.45, f32[16,20,64]{2,1,0:T(8,128)S(1)} %get-tuple-element.38, f32[16,20]{1,0:T(8,128)S(1)} %bitcast.146, f32[16,128]{1,0:T(8,128)S(1)} %get-tuple-element.46, f32[16,20,64]{2,1,0:T(8,128)S(1)} %get-tuple-element.39, ...), kind=kOutput, calls=%fused_computation.12 | convolution fusion | flops 68157440 | bytes 5694480 | tf_op jit(solution)/shard_map/rhpn,rn->rhp/dot_general | solution.py:43
  245.7 0.2 fusion.29
  245.9 0.1 pad_maximum_fusion
  245.9 0.1 copy.63
  246.0 0.2 reshape.341
  246.2 4.3 multiply_reduce_fusion.1
  250.6 5.7 psum.14
  256.2 5.1 fusion.36
  261.3 0.0 all-reduce.3.cloned.1.call-update
  261.3 0.3 all-gather.3.cloned.1.call-start
  261.6 0.3 all-gather.3.cloned.1.call-update
  261.9 0.1 gt.11
  262.0 0.8 dynamic_slice.26
  262.8 0.1 fusion.39
  262.9 0.6 pad_maximum_fusion.2
  263.6 0.2 fusion.22
  263.8 0.7 pad_maximum_fusion.1
  264.4 15.7 fusion.3
  280.1 14.6 all-reduce.3.cloned.1.call-done
  294.7 1.3 multiply_reduce_fusion
  296.0 1185.6 %all-gather.3.cloned.1.call-done = bf16[8,1572,2560]{2,1,0:T(8,128)(2,1)} async-done(((bf16[1,1572,2560]{2,1,0:T(8,128)(2,1)}), bf16[8,1572,2560]{2,1,0:T(8,128)(2,1)}) %all-gather.3.cloned.1.call-update) | async-done | bytes 64389136 | tf_op jit(solution)/shard_map/all_gather | solution.py:161
  1481.6 57.2 %reshape.415 = bf16[12576,2560]{1,0:T(8,128)(2,1)} reshape(bf16[8,1572,2560]{2,1,0:T(8,128)(2,1)} %all-gather.3.cloned.1.call-done) | data formatting | bytes 128778240
  1538.8 26.9 %select_reduce_fusion = (f32[64]{0:T(128)S(1)}, f32[64]{0:T(128)S(1)}) fusion(s32[12576]{0:T(1024)S(1)} %fusion.51, s32[64]{0:T(128)S(1)} %dynamic_slice.26, bf16[12576,2560]{1,0:T(8,128)(2,1)} %reshape.415, f32[64,2560]{1,0:T(8,128)S(1)} %copy-done.3, bf16[64,2560]{1,0:T(8,128)(2,1)S(1)} %copy-done.2, f32[2560]{0:T(1024)S(1)} %copy-done.4, ...), kind=kOutput, calls=%fused_computation.29 | convolution fusion | flops 4124942336 | bytes 65433728 | tf_op jit(solution)/shard_map/dot_general | solution.py:162
  1565.7 6.5 all-reduce
  1572.2 0.6 dynamic-slice_select_fusion
  (66 shorter events, 0.5 us)
Async XLA Ops:
  8.0 41.8 %copy-start = (bf16[2560,256]{1,0:T(8,128)(2,1)S(1)}, bf16[2560,256]{1,0:T(8,128)(2,1)}, u32[]{:S(2)}) copy-start(bf16[2560,256]{1,0:T(8,128)(2,1)} %param.31) | copy-start | bytes 3932164
  14.8 16.0 %all-to-all-start.2 = ((bf16[16,3,256]{2,1,0:T(4,128)(2,1)}), bf16[16,3,256]{2,1,0:T(4,128)(2,1)S(1)}, u32[]{:S(2)}, u32[]{:S(2)}) async-start(bf16[16,3,256]{2,1,0:T(4,128)(2,1)} %copy.59), calls=%async_computation.2 | async-start | bytes 65536 | tf_op jit(solution)/shard_map/all_to_all | solution.py:101
  30.8 13.6 all-to-all-start.1
  36.7 12.4 copy-start.2
  36.8 12.6 copy-start.12
  36.8 12.6 copy-start.13
  42.2 12.2 copy-start.10
  42.2 14.8 copy-start.5
  42.2 14.9 copy-start.14
  42.2 14.9 copy-start.7
  42.3 14.9 copy-start.8
  42.3 15.0 copy-start.9
  44.3 118.7 %all-to-all-start = ((bf16[16,20,64,128]{3,2,1,0:T(8,128)(2,1)}), bf16[16,20,64,128]{3,2,1,0:T(8,128)(2,1)}, u32[]{:S(2)}, u32[]{:S(2)}) async-start(bf16[16,20,64,128]{3,2,1,0:T(8,128)(2,1)} %broadcast_select_fusion.1), calls=%async_computation | async-start | bytes 10485760 | tf_op jit(solution)/shard_map/all_to_all | solution.py:99
  49.0 245.7 %all-reduce.3.cloned.1.call-start = ((), (), s32[]{:S(2)}) async-start(), calls=%async_computation.3 | async-start | bytes 1310720 | tf_op jit(solution)/shard_map/psum | solution.py:153
  169.1 14.9 slice-start
  169.1 14.9 slice-start.1
  222.1 23.6 %copy-start.11 = (f32[20]{0:T(128)S(1)}, f32[20]{0:T(128)}, u32[]{:S(2)}) copy-start(f32[20]{0:T(128)} %param.37) | copy-start | bytes 244
  245.7 10.5 copy-start.6
  261.3 1220.3 %all-gather.3.cloned.1.call-start = ((), (), s32[]{:S(2)}) async-start(), calls=%async_computation.4 | async-start | bytes 72622080 | tf_op jit(solution)/shard_map/all_gather | solution.py:161
  296.0 1242.8 %copy-start.3 = (f32[64,2560]{1,0:T(8,128)S(1)}, f32[64,2560]{1,0:T(8,128)}, u32[]{:S(2)}) copy-start(f32[64,2560]{1,0:T(8,128)} %all-reduce.3.cloned.1.call-done) | copy-start | bytes 1966084
  296.0 1242.8 %copy-start.4 = (f32[2560]{0:T(1024)S(1)}, f32[2560]{0:T(1024)}, u32[]{:S(2)}) copy-start(f32[2560]{0:T(1024)} %param.40) | copy-start | bytes 30724
  1538.8 34.0 %copy-start.1 = (bf16[2560,256]{1,0:T(8,128)(2,1)S(1)}, bf16[2560,256]{1,0:T(8,128)(2,1)}, u32[]{:S(2)}) copy-start(bf16[2560,256]{1,0:T(8,128)(2,1)} %param.31) | copy-start | bytes 3932164
Sparse Core Ops, SparseCore 0:
  261.4 33.2 all-reduce.2
Sparse Core Ops, SparseCore 1:
  263.3 1218.2 all-gather.2
where the time goes:
time: 1580 us
  waiting for transfers between devices  1310 us (83%)
  matrix products  118 us (7%)
  local copies, waits for them, and re-layouts  77 us (5%)
  other arithmetic  33.4 us (2%)
  starting transfers between devices  18.4 us (1%)
  between operations  16 us (1%)
    all_gather x1, waiting for transfers between devices, on_device(): piece = lax.all_gather(embedding, 'req', axis=0, tiled=True)  1190 us
    all_to_all x1, waiting for transfers between devices, on_device(): lax.all_to_all(outgoing[0], 'req', split_axis=0, concat_axis=0, tiled=True)  103 us
    dot_general x4, matrix products, run_slots(): jnp.einsum('rhpn,rn->rhp', state, reads[:, slot_index].astype(jnp.float32...  76.5 us
    unnamed x37, local copies, waits for them, and re-layouts  57.3 us
  transfers between devices with their start and end apart: 5, of which 4 were waited for; matrix products, arithmetic and copies ran while one was open for 3% of the time, Pallas kernels for 0%

commit v1 on v0

--- a/solution.py
+++ b/solution.py
@@ -158,7 +158,18 @@
     hidden_rms = jnp.where(live_share, scale_share, 0.0)
     my_ids = lax.dynamic_slice_in_dim(draft_ids, req_index * rows_dev, rows_dev)
     start_rows = jnp.full((rows_dev,), lowest, jnp.float32)
-    piece = lax.all_gather(embedding, "req", axis=0, tiled=True)
+    peers, index, extent = (lax.axis_size("req"), lax.axis_index("req"), embedding.shape[0])
+    upward = [(i, (i + 1) % peers) for i in range(peers)]
+    out = jnp.zeros(
+        (*embedding.shape[:0], peers * extent, *embedding.shape[0 + 1 :]), embedding.dtype
+    )
+    current_2 = embedding
+    for step in range(peers):
+        owner = (index - step) % peers
+        out = lax.dynamic_update_slice_in_dim(out, current_2, owner * extent, axis=0)
+        if step < peers - 1:
+            current_2 = lax.ppermute(current_2, "req", upward)
+    piece = out
     logits = lax.dot_general(
         final_rows, piece, (((1,), (1,)), ((), ())), preferred_element_type=jnp.float32
     )

time: 1580 us -> 1750 us (1.11)
  local copies, waits for them, and re-layouts: 77 us -> 307 us
  waiting for transfers between devices: 1310 us -> 1230 us
    all_gather x1 -> x0, waiting for transfers between devices: 1190 us -> none  [on_device(): piece = lax.all_gather(embedding, 'req', axis=0, tiled=True)]
    ppermute x0 -> x7, waiting for transfers between devices: none -> 898 us  [on_device(): current_2 = lax.ppermute(current_2, 'req', upward)]
    dynamic_update_slice x0 -> x8, local copies, waits for them, and re-layouts: none -> 258 us  [on_device(): lax.dynamic_update_slice_in_dim(out, current_2, owner * extent, axis=0)]
    psum x1, waiting for transfers between devices: 14.6 us -> 181 us  [on_device(): lax.psum(jnp.dot(gated_normed, out_weight, preferred_element_type=jnp.flo...]
    all_to_all x1, waiting for transfers between devices: 0.01 us -> 154 us  [on_device(): lax.all_to_all(outgoing[2], 'req', split_axis=0, concat_axis=0, tiled=True)]
    all_to_all x1, waiting for transfers between devices: 103 us -> 0.01 us  [on_device(): lax.all_to_all(outgoing[0], 'req', split_axis=0, concat_axis=0, tiled=True)]
    unnamed x37 -> x42, local copies, waits for them, and re-layouts: 57.3 us -> 9.56 us
    broadcast_in_dim x0 -> x1, local copies, waits for them, and re-layouts: none -> 20.2 us  [on_device(): jnp.zeros((*embedding.shape[:0], peers * extent, *embedding.shape[0 + 1:]...]
  transfers between devices with their start and end apart: 5 -> 11, of which waited for: 4 -> 8; matrix products, arithmetic and copies ran while one was open for 3% -> 22% of each run, Pallas kernels for 0% -> 0%
where the time goes in v1:
time: 1750 us; the launch traced here: 1740 us
  waiting for transfers between devices  1230 us (70%)
  local copies, waits for them, and re-layouts  307 us (18%)
  matrix products  118 us (7%)
  other arithmetic  33.3 us (2%)
  starting transfers between devices  19 us (1%)
    ppermute x7, waiting for transfers between devices, on_device(): current_2 = lax.ppermute(current_2, 'req', upward)  898 us
    dynamic_update_slice x8, local copies, waits for them, and re-layouts, on_device(): lax.dynamic_update_slice_in_dim(out, current_2, owner * extent, axis=0)  258 us
    psum x1, waiting for transfers between devices, on_device(): lax.psum(jnp.dot(gated_normed, out_weight, preferred_element_type=jnp.flo...  181 us
    all_to_all x1, waiting for transfers between devices, on_device(): lax.all_to_all(outgoing[2], 'req', split_axis=0, concat_axis=0, tiled=True)  154 us
    dot_general x4, matrix products, run_slots(): jnp.einsum('rhpn,rn->rhp', state, reads[:, slot_index].astype(jnp.float32...  76.5 us
  transfers between devices with their start and end apart: 11, of which 8 were waited for; matrix products, arithmetic and copies ran while one was open for 22% of the time, Pallas kernels for 0%

profile of v1, /device:TPU:0, one launch (start us, length us, event | category | flops | bytes accessed | tf_op | source)
XLA Modules:
  0.0 1738.6 jit_solution(15165932576607339945)
XLA Ops:
  7.2 3.0 collective-permute-start
  10.2 176.9 %collective-permute-done = bf16[1572,2560]{1,0:T(8,128)(2,1)S(1)} collective-permute-done((bf16[1572,2560]{1,0:T(8,128)(2,1)}, bf16[1572,2560]{1,0:T(8,128)(2,1)S(1)}, u32[]{:S(2)}, u32[]{:S(2)}) %collective-permute-start) | collective-permute-done | bytes 8048672 | tf_op jit(solution)/shard_map/ppermute | solution.py:171
  187.1 3.1 copy-done.4
  190.2 174.4 %collective-permute-done.1 = bf16[1572,2560]{1,0:T(8,128)(2,1)S(1)} collective-permute-done((bf16[1572,2560]{1,0:T(8,128)(2,1)S(1)}, bf16[1572,2560]{1,0:T(8,128)(2,1)S(1)}, u32[]{:S(2)}, u32[]{:S(2)}) %collective-permute-start.1) | collective-permute-done | bytes 8048672 | tf_op jit(solution)/shard_map/ppermute | solution.py:171
  364.6 3.2 copy-done.2
  367.7 176.6 %collective-permute-done.2 = bf16[1572,2560]{1,0:T(8,128)(2,1)S(1)} collective-permute-done((bf16[1572,2560]{1,0:T(8,128)(2,1)S(1)}, bf16[1572,2560]{1,0:T(8,128)(2,1)S(1)}, u32[]{:S(2)}, u32[]{:S(2)}) %collective-permute-start.2) | collective-permute-done | bytes 8048672 | tf_op jit(solution)/shard_map/ppermute | solution.py:171
  544.3 3.1 copy-done.3
  547.4 175.8 %collective-permute-done.3 = bf16[1572,2560]{1,0:T(8,128)(2,1)} collective-permute-done((bf16[1572,2560]{1,0:T(8,128)(2,1)S(1)}, bf16[1572,2560]{1,0:T(8,128)(2,1)}, u32[]{:S(2)}, u32[]{:S(2)}) %collective-permute-start.3) | collective-permute-done | bytes 8048672 | tf_op jit(solution)/shard_map/ppermute | solution.py:171
  723.2 3.2 sort.62
  726.5 1.2 sort.63
  727.7 1.4 gather_fusion.4
  729.2 0.6 copy.59
  729.8 6.0 all-to-all-start.2
  735.8 1.8 gather_fusion.2
  737.7 0.8 copy.55
  738.5 6.1 gather_fusion
  744.6 154.1 %all-to-all-done.2 = bf16[16,3,256]{2,1,0:T(4,128)(2,1)S(1)} async-done(((bf16[16,3,256]{2,1,0:T(4,128)(2,1)}), bf16[16,3,256]{2,1,0:T(4,128)(2,1)S(1)}, u32[]{:S(2)}, u32[]{:S(2)}) %all-to-all-start.2) | async-done | bytes 24608 | tf_op jit(solution)/shard_map/all_to_all | solution.py:101
  898.7 3.4 all-to-all-start.1
  902.1 5.5 broadcast_select_fusion.1
  907.5 2.0 all-to-all-done.1
  909.5 4.7 all-to-all-start
  914.3 1.9 collective-permute-start.5
  916.2 0.2 fusion.19
  916.4 4.2 convolution_convert_fusion.1
  920.6 0.3 fusion.18
  921.0 0.4 convolution_convert_fusion.2
  921.7 1.2 sort.64
  923.0 1.2 sort.65
  924.2 20.2 %broadcast_in_dim.40 = bf16[12576,2560]{1,0:T(8,128)(2,1)} broadcast(bf16[]{:T(256)} %constant.164.clone.1), dimensions={} | broadcast | bytes 64389120 | tf_op jit(solution)/shard_map/broadcast_in_dim | solution.py:163
  944.4 32.2 %dynamic_update_slice.24 = bf16[12576,2560]{1,0:T(8,128)(2,1)} dynamic-update-slice(bf16[12576,2560]{1,0:T(8,128)(2,1)} %broadcast_in_dim.40, bf16[1572,2560]{1,0:T(8,128)(2,1)} %param.41, s32[]{:T(128)S(6)} %select_n.138, s32[]{:T(128)} %constant.152.clone.1) | dynamic-update-slice | bytes 16097284 | tf_op jit(solution)/shard_map/dynamic_update_slice | solution.py:169
  976.7 0.8 dynamic_slice.26
  977.8 0.6 gather_fusion.5
  978.7 0.6 pad_maximum_fusion.2
  979.3 0.7 gather_fusion.3
  980.0 0.1 broadcast_select_fusion.2
  980.2 194.0 %collective-permute-done.5 = bf16[1572,2560]{1,0:T(8,128)(2,1)} collective-permute-done((bf16[1572,2560]{1,0:T(8,128)(2,1)}, bf16[1572,2560]{1,0:T(8,128)(2,1)}, u32[]{:S(2)}, u32[]{:S(2)}) %collective-permute-start.5) | collective-permute-done | bytes 8048672 | tf_op jit(solution)/shard_map/ppermute | solution.py:171
  1174.3 0.2 multiply_convert_fusion.3
  1174.5 0.3 reshape.339
  1174.7 0.2 fusion.22
  1174.9 0.7 pad_maximum_fusion.1
  1175.6 0.3 convert_multiply_fusion.11
  1175.9 32.1 %dynamic_update_slice.25 = bf16[12576,2560]{1,0:T(8,128)(2,1)} dynamic-update-slice(bf16[12576,2560]{1,0:T(8,128)(2,1)} %dynamic_update_slice.24, bf16[1572,2560]{1,0:T(8,128)(2,1)} %copy-done.4, s32[]{:T(128)S(6)} %select_n.140, s32[]{:T(128)} %constant.152.clone.1) | dynamic-update-slice | bytes 16097284 | tf_op jit(solution)/shard_map/dynamic_update_slice | solution.py:169
  1208.0 6.1 gather_fusion.1
  1214.1 14.9 fusion
  1229.0 17.5 %fusion.1 = f32[16,1,20,64]{3,1,2,0:T(1,128)S(1)} fusion(f32[16,128]{1,0:T(8,128)S(1)} %get-tuple-element.47, f32[16,20,64]{2,1,0:T(8,128)S(1)} %get-tuple-element.40, f32[16,128]{1,0:T(8,128)S(1)} %get-tuple-element.48, f32[16,20,64]{2,1,0:T(8,128)S(1)} %get-tuple-element.37, f32[16,20]{1,0:T(8,128)S(1)} %bitcast.136, f32[16,20]{1,0:T(8,128)S(1)} %bitcast.140, ...), kind=kOutput, calls=%fused_computation.11 | convolution fusion | flops 52428800 | bytes 5511696 | tf_op jit(solution)/shard_map/rhpn,rn->rhp/dot_general | solution.py:43
  1246.5 20.6 %fusion.16 = f32[16,1,20,64]{3,1,2,0:T(1,128)S(1)} fusion(f32[16,128]{1,0:T(8,128)S(1)} %get-tuple-element.46, f32[16,20,64]{2,1,0:T(8,128)S(1)} %get-tuple-element.39, f32[16,128]{1,0:T(8,128)S(1)} %get-tuple-element.47, f32[16,20,64]{2,1,0:T(8,128)S(1)} %get-tuple-element.40, f32[16,128]{1,0:T(8,128)S(1)} %get-tuple-element.48, ...), kind=kOutput, calls=%fused_computation.28 | convolution fusion | flops 60293120 | bytes 5603088 | tf_op jit(solution)/shard_map/rhpn,rn->rhp/dot_general | solution.py:43
  1267.1 23.6 %fusion.2 = f32[16,1,20,64]{3,1,2,0:T(1,128)S(1)} fusion(f32[16,128]{1,0:T(8,128)S(1)} %get-tuple-element.45, f32[16,20,64]{2,1,0:T(8,128)S(1)} %get-tuple-element.38, f32[16,20]{1,0:T(8,128)S(1)} %bitcast.144, f32[16,128]{1,0:T(8,128)S(1)} %get-tuple-element.46, f32[16,20,64]{2,1,0:T(8,128)S(1)} %get-tuple-element.39, ...), kind=kOutput, calls=%fused_computation.12 | convolution fusion | flops 68157440 | bytes 5694480 | tf_op jit(solution)/shard_map/rhpn,rn->rhp/dot_general | solution.py:43
  1290.7 0.2 fusion.29
  1291.0 0.2 reshape.341
  1291.2 4.3 multiply_reduce_fusion.1
  1295.5 6.3 psum.14
  1301.8 5.0 fusion.36
  1306.9 15.7 fusion.3
  1322.6 181.0 %all-reduce.3.cloned.1.call-done = f32[64,2560]{1,0:T(8,128)} async-done(((f32[64,2560]{1,0:T(8,128)}), f32[64,2560]{1,0:T(8,128)}) %all-reduce.3.cloned.1.call-update) | async-done | bytes 655376 | tf_op jit(solution)/shard_map/psum | solution.py:153
  1503.6 1.3 multiply_reduce_fusion
  1504.9 32.2 %dynamic_update_slice.26 = bf16[12576,2560]{1,0:T(8,128)(2,1)} dynamic-update-slice(bf16[12576,2560]{1,0:T(8,128)(2,1)} %dynamic_update_slice.25, bf16[1572,2560]{1,0:T(8,128)(2,1)} %copy-done.2, s32[]{:T(128)S(6)} %select_n.142, s32[]{:T(128)} %constant.152.clone.1) | dynamic-update-slice | bytes 16097284 | tf_op jit(solution)/shard_map/dynamic_update_slice | solution.py:169
  1537.1 32.2 %dynamic_update_slice.27 = bf16[12576,2560]{1,0:T(8,128)(2,1)} dynamic-update-slice(bf16[12576,2560]{1,0:T(8,128)(2,1)} %dynamic_update_slice.26, bf16[1572,2560]{1,0:T(8,128)(2,1)} %copy-done.3, s32[]{:T(128)S(6)} %select_n.144, s32[]{:T(128)} %constant.152.clone.1) | dynamic-update-slice | bytes 16097284 | tf_op jit(solution)/shard_map/dynamic_update_slice | solution.py:169
  1569.4 32.2 %dynamic_update_slice.28 = bf16[12576,2560]{1,0:T(8,128)(2,1)} dynamic-update-slice(bf16[12576,2560]{1,0:T(8,128)(2,1)} %dynamic_update_slice.27, bf16[1572,2560]{1,0:T(8,128)(2,1)} %collective-permute-done.3, s32[]{:T(128)S(6)} %select_n.146, s32[]{:T(128)} %constant.152.clone.1) | dynamic-update-slice | bytes 16097284 | tf_op jit(solution)/shard_map/dynamic_update_slice | solution.py:169
  1601.6 32.2 %dynamic_update_slice.29 = bf16[12576,2560]{1,0:T(8,128)(2,1)} dynamic-update-slice(bf16[12576,2560]{1,0:T(8,128)(2,1)} %dynamic_update_slice.28, bf16[1572,2560]{1,0:T(8,128)(2,1)} %collective-permute-done.4, s32[]{:T(128)S(6)} %select_n.148, s32[]{:T(128)} %constant.152.clone.1) | dynamic-update-slice | bytes 16097284 | tf_op jit(solution)/shard_map/dynamic_update_slice | solution.py:169
  1633.8 32.2 %dynamic_update_slice.30 = bf16[12576,2560]{1,0:T(8,128)(2,1)} dynamic-update-slice(bf16[12576,2560]{1,0:T(8,128)(2,1)} %dynamic_update_slice.29, bf16[1572,2560]{1,0:T(8,128)(2,1)} %collective-permute-done.5, s32[]{:T(128)S(6)} %select_n.150, s32[]{:T(128)} %constant.152.clone.1) | dynamic-update-slice | bytes 16097284 | tf_op jit(solution)/shard_map/dynamic_update_slice | solution.py:169
  1666.1 32.3 %dynamic_update_slice.31 = bf16[12576,2560]{1,0:T(8,128)(2,1)} dynamic-update-slice(bf16[12576,2560]{1,0:T(8,128)(2,1)} %dynamic_update_slice.30, bf16[1572,2560]{1,0:T(8,128)(2,1)} %collective-permute-done.6, s32[]{:T(128)S(6)} %select_n.152, s32[]{:T(128)} %constant.152.clone.1) | dynamic-update-slice | bytes 16097284 | tf_op jit(solution)/shard_map/dynamic_update_slice | solution.py:169
  1698.3 27.0 %select_reduce_fusion = (f32[64]{0:T(128)S(1)}, f32[64]{0:T(128)S(1)}) fusion(s32[12576]{0:T(1024)S(1)} %fusion.51, s32[64]{0:T(128)S(1)} %dynamic_slice.26, bf16[12576,2560]{1,0:T(8,128)(2,1)} %dynamic_update_slice.31, f32[64,2560]{1,0:T(8,128)S(1)} %copy-done.6, bf16[64,2560]{1,0:T(8,128)(2,1)S(1)} %copy-done.5, f32[2560]{0:T(1024)S(1)} %copy-done.7, ...), kind=kOutput, calls=%fused_computation.29 | convolution fusion | flops 4124942336 | bytes 65433728 | tf_op jit(solution)/shard_map/dot_general | solution.py:173
  1725.4 5.8 all-reduce
  1731.1 0.6 dynamic-slice_select_fusion
  (91 shorter events, 1.6 us)
Async XLA Ops:
  7.2 913.8 %copy-start = (bf16[2560,256]{1,0:T(8,128)(2,1)S(1)}, bf16[2560,256]{1,0:T(8,128)(2,1)}, u32[]{:S(2)}) copy-start(bf16[2560,256]{1,0:T(8,128)(2,1)} %param.31) | copy-start | bytes 3932164
  7.2 179.9 %collective-permute-start = (bf16[1572,2560]{1,0:T(8,128)(2,1)}, bf16[1572,2560]{1,0:T(8,128)(2,1)S(1)}, u32[]{:S(2)}, u32[]{:S(2)}) collective-permute-start(bf16[1572,2560]{1,0:T(8,128)(2,1)} %param.41), channel_id=1, source_target_pairs={{0,4},{4,8},{8,12},{12,16},{16,20},{20,24},{24,28},{28,0},{1,5},{5... | collective-permute-start | bytes 24145928 | tf_op jit(solution)/shard_map/ppermute | solution.py:171
  187.1 3.1 copy-start.4
  187.1 177.5 %collective-permute-start.1 = (bf16[1572,2560]{1,0:T(8,128)(2,1)S(1)}, bf16[1572,2560]{1,0:T(8,128)(2,1)S(1)}, u32[]{:S(2)}, u32[]{:S(2)}) collective-permute-start(bf16[1572,2560]{1,0:T(8,128)(2,1)S(1)} %collective-permute-done), channel_id=1, source_target_pairs={{0,4},{4,8},{8,12},{12,16},{16,20},{20,24},{24,28},{28,0},{1,5},{5... | collective-permute-start | bytes 24145928 | tf_op jit(solution)/shard_map/ppermute | solution.py:171
  364.6 3.2 copy-start.2
  367.7 176.6 %collective-permute-start.2 = (bf16[1572,2560]{1,0:T(8,128)(2,1)S(1)}, bf16[1572,2560]{1,0:T(8,128)(2,1)S(1)}, u32[]{:S(2)}, u32[]{:S(2)}) collective-permute-start(bf16[1572,2560]{1,0:T(8,128)(2,1)S(1)} %collective-permute-done.1), channel_id=1, source_target_pairs={{0,4},{4,8},{8,12},{12,16},{16,20},{20,24},{24,28},{28,0},{1,5},{5... | collective-permute-start | bytes 24145928 | tf_op jit(solution)/shard_map/ppermute | solution.py:171
  544.3 3.1 copy-start.3
  547.4 175.8 %collective-permute-start.3 = (bf16[1572,2560]{1,0:T(8,128)(2,1)S(1)}, bf16[1572,2560]{1,0:T(8,128)(2,1)}, u32[]{:S(2)}, u32[]{:S(2)}) collective-permute-start(bf16[1572,2560]{1,0:T(8,128)(2,1)S(1)} %collective-permute-done.2), channel_id=1, source_target_pairs={{0,4},{4,8},{8,12},{12,16},{16,20},{20,24},{24,28},{28,0},{1,5},{5... | collective-permute-start | bytes 24145928 | tf_op jit(solution)/shard_map/ppermute | solution.py:171
  723.2 191.1 %collective-permute-start.4 = (bf16[1572,2560]{1,0:T(8,128)(2,1)}, bf16[1572,2560]{1,0:T(8,128)(2,1)}, u32[]{:S(2)}, u32[]{:S(2)}) collective-permute-start(bf16[1572,2560]{1,0:T(8,128)(2,1)} %collective-permute-done.3), channel_id=1, source_target_pairs={{0,4},{4,8},{8,12},{12,16},{16,20},{20,24},{24,28},{28,0},{1,5},{5... | collective-permute-start | bytes 24145928 | tf_op jit(solution)/shard_map/ppermute | solution.py:171
  729.8 168.8 %all-to-all-start.2 = ((bf16[16,3,256]{2,1,0:T(4,128)(2,1)}), bf16[16,3,256]{2,1,0:T(4,128)(2,1)S(1)}, u32[]{:S(2)}, u32[]{:S(2)}) async-start(bf16[16,3,256]{2,1,0:T(4,128)(2,1)} %copy.59), calls=%async_computation.2 | async-start | bytes 65536 | tf_op jit(solution)/shard_map/all_to_all | solution.py:101
  898.7 10.9 all-to-all-start.1
  902.0 14.1 copy-start.5
  902.1 14.3 copy-start.16
  907.5 13.1 copy-start.15
  907.5 13.9 copy-start.11
  907.5 14.1 copy-start.13
  909.5 298.5 %all-to-all-start = ((bf16[16,20,64,128]{3,2,1,0:T(8,128)(2,1)}), bf16[16,20,64,128]{3,2,1,0:T(8,128)(2,1)}, u32[]{:S(2)}, u32[]{:S(2)}) async-start(bf16[16,20,64,128]{3,2,1,0:T(8,128)(2,1)} %broadcast_select_fusion.1), calls=%async_computation | async-start | bytes 10485760 | tf_op jit(solution)/shard_map/all_to_all | solution.py:99
  914.2 589.4 %all-reduce.3.cloned.1.call-start = ((), (), s32[]{:S(2)}) async-start(), calls=%async_computation.3 | async-start | bytes 1310720 | tf_op jit(solution)/shard_map/psum | solution.py:153
  914.3 260.0 %collective-permute-start.5 = (bf16[1572,2560]{1,0:T(8,128)(2,1)}, bf16[1572,2560]{1,0:T(8,128)(2,1)}, u32[]{:S(2)}, u32[]{:S(2)}) collective-permute-start(bf16[1572,2560]{1,0:T(8,128)(2,1)} %collective-permute-done.4), channel_id=1, source_target_pairs={{0,4},{4,8},{8,12},{12,16},{16,20},{20,24},{24,28},{28,0},{1,5},{5... | collective-permute-start | bytes 24145928 | tf_op jit(solution)/shard_map/ppermute | solution.py:171
  944.4 33.0 %copy-start.8 = (bf16[4,1280]{1,0:T(4,128)(2,1)S(1)}, bf16[4,1280]{1,0:T(4,128)(2,1)}, u32[]{:S(2)}) copy-start(bf16[4,1280]{1,0:T(4,128)(2,1)} %param.33) | copy-start | bytes 30724
  944.4 33.1 %copy-start.17 = (f32[20]{0:T(128)S(1)}, f32[20]{0:T(128)}, u32[]{:S(2)}) copy-start(f32[20]{0:T(128)} %param.35) | copy-start | bytes 244
  944.4 33.2 %copy-start.10 = (bf16[4,256]{1,0:T(4,128)(2,1)S(1)}, bf16[4,256]{1,0:T(4,128)(2,1)}, u32[]{:S(2)}) copy-start(bf16[4,256]{1,0:T(4,128)(2,1)} %param.34) | copy-start | bytes 6148
  944.4 33.2 %copy-start.12 = (f32[20]{0:T(128)S(1)}, f32[20]{0:T(128)}, u32[]{:S(2)}) copy-start(f32[20]{0:T(128)} %param.36) | copy-start | bytes 244
  1174.3 491.8 %collective-permute-start.6 = (bf16[1572,2560]{1,0:T(8,128)(2,1)}, bf16[1572,2560]{1,0:T(8,128)(2,1)}, u32[]{:S(2)}, u32[]{:S(2)}) collective-permute-start(bf16[1572,2560]{1,0:T(8,128)(2,1)} %collective-permute-done.5), channel_id=1, source_target_pairs={{0,4},{4,8},{8,12},{12,16},{16,20},{20,24},{24,28},{28,0},{1,5},{5... | collective-permute-start | bytes 24145928 | tf_op jit(solution)/shard_map/ppermute | solution.py:171
  1214.1 14.9 slice-start
  1214.1 14.9 slice-start.1
  1267.1 23.6 %copy-start.14 = (f32[20]{0:T(128)S(1)}, f32[20]{0:T(128)}, u32[]{:S(2)}) copy-start(f32[20]{0:T(128)} %param.37) | copy-start | bytes 244
  1290.7 11.2 copy-start.9
  1666.0 32.3 %copy-start.6 = (f32[64,2560]{1,0:T(8,128)S(1)}, f32[64,2560]{1,0:T(8,128)}, u32[]{:S(2)}) copy-start(f32[64,2560]{1,0:T(8,128)} %all-reduce.3.cloned.1.call-done) | copy-start | bytes 1966084
  1666.0 32.3 %copy-start.7 = (f32[2560]{0:T(1024)S(1)}, f32[2560]{0:T(1024)}, u32[]{:S(2)}) copy-start(f32[2560]{0:T(1024)} %param.40) | copy-start | bytes 30724
  1698.3 33.4 %copy-start.1 = (bf16[2560,256]{1,0:T(8,128)(2,1)S(1)}, bf16[2560,256]{1,0:T(8,128)(2,1)}, u32[]{:S(2)}) copy-start(bf16[2560,256]{1,0:T(8,128)(2,1)} %param.31) | copy-start | bytes 3932164
Sparse Core Ops, SparseCore 0:
  1307.0 196.5 all-reduce.2
